TPU v7x, 512 devices: a whole 4x4x16 slice. The times are simulated.
512 devices in a mesh: fsdp: 32 (over x, z_hi, core), ctx: 16 (over y, z_lo).
Axes of the slice: x: 4, y: 4, z: 16 (z_hi: 4, z_lo: 4; z = z_hi * 4 + z_lo), core: 2. Of those that a mesh axis runs over, the one named last changes fastest.
Arguments:
- features: bfloat16 [3, 16384, 8192], P(None, 'ctx', 'fsdp'), may hold values from -6 to 6
- short_taps: float32 [3, 3, 8192], P(None, None, 'fsdp'), may hold values from -3.5 to 3.5
- decay_rates: float32 [512, 16], P('fsdp'), may hold values from 1.5258789e-05 to 0.1
- mode_gains: float32 [512, 16], P('fsdp'), may hold values from -2.5 to 2.5
- cotangent: bfloat16 [16384, 8192], P('ctx', 'fsdp'), may hold values from -6 to 6
Outputs:
- mixer_output: bfloat16 [16384, 8192], P('ctx', 'fsdp')
- feature_grads: bfloat16 [3, 16384, 8192], P(None, 'ctx', 'fsdp')
- gain_grads: float32 [512, 16], P('fsdp')
- rate_grads: float32 [512, 16], P('fsdp')
All inputs are finite; a program needn't handle non-finite values.
Results may differ from a plain program's by a relative error of at most 0.0048.
Values may be sent and summed in bfloat16 or wider, within the bound.
A program may use at most 64 MiB of HBM per device.

v0:
```python
import jax
import jax.numpy as jnp
from jax import lax
from jax.sharding import PartitionSpec as P

precise = lax.Precision.HIGHEST
threepass = lax.Precision.HIGH


def passed_along(value, axis, steps):
    count = lax.axis_size(axis)
    leading, last = (max(0, -steps), min(count, count - steps))
    return lax.ppermute(value, axis, [(source, source + steps) for source in range(leading, last)])


def diagonal_sums(gram_acc):
    group_count, block_len, width_same = gram_acc.shape
    flipped = jnp.flip(gram_acc, axis=2)
    padded = jnp.concatenate([flipped, jnp.zeros_like(flipped)], axis=2)
    flattened = padded.reshape(group_count, 2 * block_len * block_len)[
        :, : block_len * (2 * block_len - 1)
    ]
    sheared = flattened.reshape(group_count, block_len, 2 * block_len - 1)
    return jnp.sum(sheared, axis=1)[:, block_len - 1 :]


def short_conv(taps_table, row_data, tokens, rim_rows, forward):
    summed = jnp.zeros((3, tokens, row_data.shape[2]), jnp.float32)
    for offset in range(taps_table.shape[1]):
        start_row = rim_rows - offset if forward else offset
        summed = (
            summed + taps_table[:, offset, None, :] * row_data[:, start_row : start_row + tokens, :]
        )
    return summed


def per_device(features, short_taps, decay_rates, mode_gains, cotangent):
    tokens = features.shape[1]
    channels = features.shape[2]
    group_count = decay_rates.shape[0]
    order_count = decay_rates.shape[1]
    members = channels // group_count
    rim_rows = short_taps.shape[1] - 1
    block_len = 128
    block_count = tokens // block_len
    ctx_count = lax.axis_size("ctx")
    ctx_index = lax.axis_index("ctx")
    earlier_rows = passed_along(features[:, tokens - rim_rows :, :], "ctx", 1)
    extended = jnp.concatenate([earlier_rows, features], axis=1)
    shaped = short_conv(short_taps, extended, tokens, rim_rows, True)
    query_part, key_part, value_part = (shaped[0], shaped[1], shaped[2])
    product = (key_part * value_part).astype(jnp.bfloat16)
    adjoint = cotangent * query_part
    grouped_z = product.reshape(tokens, group_count, members)
    grouped_e = adjoint.reshape(tokens, group_count, members)
    mode_coefs = mode_gains * jnp.sqrt(2.0 * decay_rates)
    rate_axis = decay_rates[:, :, None]
    positions = jnp.arange(tokens, dtype=jnp.float32)[None, None, :]
    decay_from = jnp.exp(-rate_axis * positions)
    end_tables = jnp.stack([jnp.flip(decay_from, 2), -jnp.flip(positions * decay_from, 2)])
    end_states = jnp.einsum(
        "kgns,sgm->kngm", end_tables, grouped_z.astype(jnp.float32), precision=threepass
    )
    start_state = jnp.einsum("gnt,tgm->ngm", decay_from, grouped_e, precision=precise)
    local_states = jnp.stack([end_states[0], end_states[1], start_state]).reshape(
        3, order_count, channels
    )
    rate_cols = jnp.repeat(decay_rates.T, members, axis=1)
    everyone = lax.all_gather(local_states[None], "ctx", axis=0, tiled=True)
    device_ids = jnp.arange(ctx_count, dtype=jnp.int32)
    ahead_steps = (ctx_index - 1 - device_ids).astype(jnp.float32)[:, None, None]
    behind_steps = (device_ids - ctx_index - 1).astype(jnp.float32)[:, None, None]
    ahead_weight = jnp.where(
        ahead_steps >= 0, jnp.exp(-rate_cols[None] * (tokens * jnp.maximum(ahead_steps, 0.0))), 0.0
    )
    behind_weight = jnp.where(
        behind_steps >= 0,
        jnp.exp(-rate_cols[None] * (tokens * jnp.maximum(behind_steps, 0.0))),
        0.0,
    )
    prev_state = jnp.sum(ahead_weight * everyone[:, 0], axis=0)
    prev_lagged = jnp.sum(
        ahead_weight * (everyone[:, 1] - tokens * ahead_steps * everyone[:, 0]), axis=0
    )
    next_state = jnp.sum(behind_weight * everyone[:, 2], axis=0)
    lag_axis = jnp.arange(block_len, dtype=jnp.float32)[None, None, :]
    block_pow = jnp.exp(-rate_axis * lag_axis)
    block_after = block_pow * jnp.exp(-rate_axis)
    block_moments = jnp.stack([block_after, (lag_axis + 1.0) * block_after])
    coef_after = mode_coefs[:, :, None] * block_after
    block_ends = jnp.stack([jnp.flip(block_pow, 2), -jnp.flip(lag_axis * block_pow, 2)])
    coef_tail = mode_coefs[:, :, None] * jnp.flip(block_after, 2)
    block_span = jnp.exp(-decay_rates * block_len).T[:, :, None]
    filter_taps = jnp.sum(mode_coefs[:, :, None] * block_pow, axis=1)
    lag_index = (
        jnp.arange(block_len, dtype=jnp.int32)[:, None]
        - jnp.arange(block_len, dtype=jnp.int32)[None, :]
    )
    toeplitz = jnp.where(lag_index[None] >= 0, filter_taps[:, jnp.maximum(lag_index, 0)], 0.0)
    z_blocks = grouped_z.reshape(block_count, block_len, group_count, members)
    e_blocks = grouped_e.reshape(block_count, block_len, group_count, members)

    def forward_block(carried_in, inputs):
        mode_state, lagged, first_acc, lag_acc, gram_acc = carried_in
        z_block, e_block = inputs
        z_wide = z_block.astype(jnp.float32)
        inside_part = jnp.einsum("gts,sgm->tgm", toeplitz, z_wide, precision=threepass)
        carried = jnp.einsum("gnt,ngm->tgm", coef_after, mode_state, precision=precise)
        moments = jnp.einsum("kgnt,tgm->kngm", block_moments, e_block, precision=precise)
        first_acc = first_acc + jnp.sum(moments[0] * mode_state, axis=2)
        lag_acc = lag_acc + jnp.sum(moments[0] * lagged - moments[1] * mode_state, axis=2)
        gram_acc = gram_acc + jnp.einsum("tgm,sgm->gts", e_block, z_wide, precision=precise)
        fresh_part = jnp.einsum("kgns,sgm->kngm", block_ends, z_wide, precision=threepass)
        new_lagged = block_span * lagged - block_len * block_span * mode_state + fresh_part[1]
        new_state = block_span * mode_state + fresh_part[0]
        return ((new_state, new_lagged, first_acc, lag_acc, gram_acc), inside_part + carried)

    zero_state = jnp.zeros((order_count, group_count, members), jnp.float32)
    zero_pairs = jnp.zeros((order_count, group_count), jnp.float32)
    zero_gram = jnp.zeros((group_count, block_len, block_len), jnp.float32)
    final_carry, inner_blocks = lax.scan(
        forward_block,
        (zero_state, zero_state, zero_pairs, zero_pairs, zero_gram),
        (z_blocks, e_blocks),
    )
    first_acc, lag_acc, gram_acc = (final_carry[2], final_carry[3], final_carry[4])

    def backward_block(later_state, e_block):
        inside_part = jnp.einsum("gts,tgm->sgm", toeplitz, e_block, precision=precise)
        carried = jnp.einsum("gns,ngm->sgm", coef_tail, later_state, precision=precise)
        fresh_part = jnp.einsum("gnt,tgm->ngm", block_pow, e_block, precision=precise)
        return (block_span * later_state + fresh_part, inside_part + carried)

    top_state, grad_blocks = lax.scan(backward_block, zero_state, e_blocks, reverse=True)
    prev_grouped = prev_state.reshape(order_count, group_count, members)
    lagged_grouped = prev_lagged.reshape(order_count, group_count, members)
    next_grouped = next_state.reshape(order_count, group_count, members)
    device_after = decay_from * jnp.exp(-rate_axis)
    inner_sum = inner_blocks.reshape(tokens, group_count, members) + jnp.einsum(
        "gnt,ngm->tgm", mode_coefs[:, :, None] * device_after, prev_grouped, precision=precise
    )
    first_moment = jnp.exp(-decay_rates).T[:, :, None] * start_state
    second_moment = jnp.einsum(
        "gnt,tgm->ngm", (positions + 1.0) * device_after, grouped_e, precision=precise
    )
    first_acc = first_acc + jnp.sum(first_moment * prev_grouped, axis=2)
    lag_acc = lag_acc + jnp.sum(
        first_moment * lagged_grouped - second_moment * prev_grouped, axis=2
    )
    device_tail = mode_coefs[:, :, None] * jnp.flip(device_after, 2)
    product_grad = grad_blocks.reshape(tokens, group_count, members) + jnp.einsum(
        "gns,ngm->sgm", device_tail, next_grouped, precision=precise
    )
    lag_totals = diagonal_sums(gram_acc)
    first_total = first_acc.T + jnp.sum(lag_totals[:, None, :] * block_pow, axis=2)
    lag_total = lag_acc.T - jnp.sum(lag_totals[:, None, :] * lag_axis * block_pow, axis=2)
    gain_part = jnp.sqrt(2.0 * decay_rates) * first_total
    rate_part = mode_coefs * (0.5 * first_total + decay_rates * lag_total)
    inner_flat = inner_sum.reshape(tokens, channels)
    mixer_output = (query_part * inner_flat).astype(jnp.bfloat16)
    grad_flat = product_grad.reshape(tokens, channels)
    feature_adj = jnp.stack([cotangent * inner_flat, grad_flat * value_part, grad_flat * key_part])
    later_rows = passed_along(feature_adj[:, :rim_rows, :], "ctx", -1)
    appended = jnp.concatenate([feature_adj, later_rows], axis=1)
    feature_grads = short_conv(short_taps, appended, tokens, rim_rows, False).astype(jnp.bfloat16)
    filter_local = jnp.stack([gain_part, rate_part])
    entry_count = 2 * group_count * order_count * lax.axis_size("fsdp")
    summed = lax.psum(filter_local, "ctx")
    squares = lax.psum(jnp.sum(summed * summed), "fsdp")
    factor = jnp.minimum(1.0, lax.rsqrt(squares / entry_count + 1e-06))
    clipped = summed * factor
    return (mixer_output, feature_grads, clipped[0], clipped[1])


def solution(mesh):
    return jax.shard_map(
        per_device,
        mesh=mesh,
        in_specs=(
            P(None, "ctx", "fsdp"),
            P(None, None, "fsdp"),
            P("fsdp", None),
            P("fsdp", None),
            P("ctx", "fsdp"),
        ),
        out_specs=(P("ctx", "fsdp"), P(None, "ctx", "fsdp"), P("fsdp", None), P("fsdp", None)),
        check_vma=False,
    )
```

profile of v0, /device:TPU:1, one launch (start us, length us, event | category | flops | bytes accessed | tf_op | source)
XLA Modules:
  0.0 575.3 jit_solution(6784911890546579179)
XLA Ops:
  2.2 5.1 collective-permute-start
  14.9 54.5 %gather_fusion = f32[16384,16]{1,0:T(8,128)} fusion(f32[16,128]{0,1:T(8,128)S(1)} %copy.59, s32[16384]{0:T(1024)S(1)} %bitcast_clamp_fusion), kind=kCustom, calls=%fused_computation | custom fusion | bytes 2162688 | tf_op jit(solution)/shard_map/gather | solution.py:99
  69.4 5.2 copy.60
  77.4 2.6 copy.55
  80.0 3.3 rev.26
  87.9 4.8 multiply_add_fusion
  95.4 3.3 fusion.63
  105.0 41.3 %all_gather.3 = f32[16,3,16,256]{3,2,1,0:T(8,128)S(1)} all-gather(f32[1,3,16,256]{3,2,1,0:T(8,128)S(1)} %pad_maximum_fusion.5), channel_id=1, replica_groups=mesh['fsdp'=32,'ctx'=16] {'ctx'}, dimensions={0}, use_global_device_ids=true | all-gather | bytes 835584 | tf_op jit(solution)/shard_map/all_gather | solution.py:69
  154.0 132.3 %while.38 = (s32[]{:T(128)}, f32[16,16,16]{0,2,1:T(8,128)S(1)}, f32[16,16,16]{0,2,1:T(8,128)}, f32[16,16]{0,1:T(8,128)}, f32[16,16]{0,1:T(8,128)}, /*index=5*/f3...) while((s32[]{:T(128)}, f32[16,16,16]{0,2,1:T(8,128)S(1)}, ...), condition=%wide.region_4.5_spmd.clone, body=%wide.region_1.0_spmd.clone.sunk | while | flops 101380864 | bytes 5014714 | solution.py:121
  156.8 2.9 convolution_bitcast_fusion.8
  162.6 4.5 dynamic_update_slice.17
  172.0 2.9 convolution_bitcast_fusion.8
  179.4 4.5 dynamic_update_slice.17
  188.7 2.9 convolution_bitcast_fusion.8
  196.1 4.5 dynamic_update_slice.17
  205.5 2.9 convolution_bitcast_fusion.8
  212.9 4.5 dynamic_update_slice.17
  222.2 2.9 convolution_bitcast_fusion.8
  229.6 4.5 dynamic_update_slice.17
  239.0 2.9 convolution_bitcast_fusion.8
  246.3 4.5 dynamic_update_slice.17
  255.7 2.9 convolution_bitcast_fusion.8
  263.1 4.5 dynamic_update_slice.17
  272.5 2.9 convolution_bitcast_fusion.8
  279.8 4.5 dynamic_update_slice.17
  286.4 5.8 %rev.30 = f32[16,128,128]{2,1,0:T(8,128)} reverse(f32[16,128,128]{2,1,0:T(8,128)S(1)} %get-tuple-element.242), dimensions={2} | reverse | bytes 2097152 | tf_op jit(solution)/shard_map/jit(_flip)/rev | solution.py:18
  296.3 6.3 %reshape.172 = f32[16,128,255]{2,1,0:T(8,128)} reshape(f32[16,32640]{1,0:T(8,128)} %slice.116) | data formatting | bytes 4177920 | tf_op jit(solution)/shard_map/reshape | solution.py:23
  302.6 2.4 reduce_sum.112
  307.9 2.6 fusion.68
  311.3 61.1 %psum.14 = f32[2,16,16]{2,1,0:T(8,128)S(1)} all-reduce(f32[2,16,16]{2,1,0:T(8,128)S(1)} %pad_maximum_fusion.6), channel_id=1, replica_groups=mesh['fsdp'=32,'ctx'=16] {'ctx'}, use_global_device_ids=true, to_apply=%region_15.16 | all-reduce | flops 512 | bytes 4096 | tf_op jit(solution)/shard_map/psum | solution.py:168
  373.0 5.5 rev.29
  378.5 108.7 %psum.15 = f32[]{:T(128)} all-reduce(f32[]{:T(128)} %multiply_reduce_fusion.6), channel_id=1, replica_groups=mesh['fsdp'=32,'ctx'=16] {'fsdp'}, use_global_device_ids=true, to_apply=%region_17.18 | all-reduce | flops 1 | bytes 8 | tf_op jit(solution)/shard_map/psum | solution.py:169
  491.4 49.0 %while.39 = (s32[]{:T(128)}, f32[16,16,16]{0,2,1:T(8,128)S(1)}, f32[8,128,16,16]{1,0,3,2:T(8,128)}, f32[16,16,1]{0,1,2:T(8,128)S(1)}, f32[8,128,16,16]{1,3,2,0:T...) while((s32[]{:T(128)}, f32[16,16,16]{0,2,1:T(8,128)S(1)}, ...), condition=%wide.region_7.8_spmd.clone, body=%wide.region_6.7_spmd.clone.sunk | while | flops 62996484 | bytes 2277520 | solution.py:134
  492.6 4.5 dynamic_update_slice.18
  498.8 4.5 dynamic_update_slice.18
  504.9 4.5 dynamic_update_slice.18
  511.0 4.5 dynamic_update_slice.18
  517.2 4.5 dynamic_update_slice.18
  523.3 4.5 dynamic_update_slice.18
  529.4 4.5 dynamic_update_slice.18
  535.5 4.5 dynamic_update_slice.18
  540.4 2.5 reshape.168
  543.0 2.6 fusion.61
  547.3 2.4 reshape.164
  549.6 2.6 fusion.62
  558.4 9.5 %collective-permute-done.1 = f32[3,2,256]{1,2,0:T(8,128)S(1)} collective-permute-done((f32[3,2,256]{1,2,0:T(8,128)S(1)}, f32[3,2,256]{1,2,0:T(8,128)S(1)}, u32[]{:S(2)}, u32[]{:S(2)}) %collective-permute-start.1) | collective-permute-done | bytes 6176 | tf_op jit(solution)/shard_map/ppermute | solution.py:13
  569.5 3.3 fusion.54
  572.8 2.6 copy.77
  (215 shorter events, 140.8 us)
Async XLA Ops:
  2.2 85.7 %collective-permute-start = (bf16[3,2,256]{1,2,0:T(8,128)(2,1)}, bf16[3,2,256]{1,2,0:T(8,128)(2,1)}, u32[]{:S(2)}, u32[]{:S(2)}) collective-permute-start(bf16[3,2,256]{1,2,0:T(8,128)(2,1)} %copy.56), channel_id=1, source_target_pairs={{0,1},{1,2},{2,3},{3,4},{4,5},{5,6},{6,7},{7,8},{8,9},{9,10},{10,1... | collective-permute-start | bytes 9224 | tf_op jit(solution)/shard_map/ppermute | solution.py:13
  10.3 4.0 copy-start.19
  10.3 4.3 copy-start.17
  10.3 3.4 copy-start.29
  76.7 6.5 %copy-start.28 = (f32[3,1,256]{2,1,0:T(1,128)S(1)}, f32[3,1,256]{2,1,0:T(1,128)}, u32[]{:S(2)}) copy-start(f32[3,1,256]{2,1,0:T(1,128)} %get-tuple-element.483) | copy-start | bytes 9220
  77.4 7.9 %copy-start.27 = (f32[16,16]{0,1:T(8,128)S(1)}, f32[16,16]{0,1:T(8,128)}, u32[]{:S(2)}) copy-start(f32[16,16]{0,1:T(8,128)} %get-tuple-element.489) | copy-start | bytes 3076
  83.2 4.6 copy-start.25
  92.7 1.6 copy-start
  92.7 2.6 copy-start.10
  92.7 2.7 copy-start.11
  102.1 49.1 %copy-start.8 = (f32[1024,256]{0,1:T(8,128)}, f32[1024,256]{0,1:T(8,128)S(1)}, u32[]{:S(2)}) copy-start(f32[1024,256]{0,1:T(8,128)S(1)} %convert_multiply_fusion.1) | copy-start | bytes 3145732
  103.6 47.8 %copy-start.15 = (f32[16,16,16]{2,1,0:T(8,128)}, f32[16,16,16]{2,1,0:T(8,128)S(1)}, u32[]{:S(2)}) copy-start(f32[16,16,16]{2,1,0:T(8,128)S(1)} %fusion.75) | copy-start | bytes 49156
  150.9 1.0 copy-start.12
  296.3 10.9 %copy-start.14 = (f32[16,256]{0,1:T(8,128)S(1)}, f32[16,256]{0,1:T(8,128)}, u32[]{:S(2)}) copy-start(f32[16,256]{0,1:T(8,128)} %copy.70) | copy-start | bytes 49156
  296.3 10.9 %copy-start.16 = (f32[16,16,16]{2,1,0:T(8,128)S(1)}, f32[16,16,16]{2,1,0:T(8,128)}, u32[]{:S(2)}) copy-start(f32[16,16,16]{2,1,0:T(8,128)} %copy-done.15) | copy-start | bytes 49156
  296.3 11.6 %copy-start.9 = (f32[1024,256]{0,1:T(8,128)S(1)}, f32[1024,256]{0,1:T(8,128)}, u32[]{:S(2)}) copy-start(f32[1024,256]{0,1:T(8,128)} %copy-done.8) | copy-start | bytes 3145732
  491.4 51.5 %copy-start.21 = (f32[16,256]{1,0:T(8,128)S(1)}, f32[16,256]{1,0:T(8,128)}, u32[]{:S(2)}) copy-start(f32[16,256]{1,0:T(8,128)} %get-tuple-element.414) | copy-start | bytes 49156
  491.4 51.6 %copy-start.20 = (f32[16,16]{1,0:T(8,128)S(1)}, f32[16,16]{1,0:T(8,128)}, u32[]{:S(2)}) copy-start(f32[16,16]{1,0:T(8,128)} %get-tuple-element.758) | copy-start | bytes 3076
  540.4 5.2 copy-start.1
  545.6 4.0 copy-start.18
  549.6 4.6 copy-start.2
  549.6 4.6 copy-start.4
  554.3 1.0 copy-start.6
  554.3 2.5 copy-start.22
  554.3 3.1 copy-start.13
  554.3 13.6 %copy-start.3 = (f32[1,1024,256]{1,2,0:T(8,128)S(1)}, f32[1,1024,256]{1,2,0:T(8,128)}, u32[]{:S(2)}) copy-start(f32[1,1024,256]{1,2,0:T(8,128)} %get-tuple-element.471) | copy-start | bytes 3145732
  554.3 13.6 %copy-start.5 = (f32[1,1024,256]{1,2,0:T(8,128)S(1)}, f32[1,1024,256]{1,2,0:T(8,128)}, u32[]{:S(2)}) copy-start(f32[1,1024,256]{1,2,0:T(8,128)} %get-tuple-element.472) | copy-start | bytes 3145732
  555.4 12.6 %collective-permute-start.1 = (f32[3,2,256]{1,2,0:T(8,128)S(1)}, f32[3,2,256]{1,2,0:T(8,128)S(1)}, u32[]{:S(2)}, u32[]{:S(2)}) collective-permute-start(f32[3,2,256]{1,2,0:T(8,128)S(1)} %slice.113), channel_id=1, source_target_pairs={{1,0},{2,1},{3,2},{4,3},{5,4},{6,5},{7,6},{8,7},{9,8},{10,9},{11,1... | collective-permute-start | bytes 18440 | tf_op jit(solution)/shard_map/ppermute | solution.py:13
  558.4 11.0 %copy-start.7 = (f32[1,1024,256]{1,2,0:T(8,128)S(1)}, f32[1,1024,256]{1,2,0:T(8,128)}, u32[]{:S(2)}) copy-start(f32[1,1024,256]{1,2,0:T(8,128)} %copy-done.6) | copy-start | bytes 3145732
  558.4 11.0 %copy-start.23 = (f32[3,256]{1,0:T(4,128)S(1)}, f32[3,256]{1,0:T(4,128)}, u32[]{:S(2)}) copy-start(f32[3,256]{1,0:T(4,128)} %get-tuple-element.499) | copy-start | bytes 9220
  558.4 11.0 %copy-start.24 = (f32[3,256]{1,0:T(4,128)S(1)}, f32[3,256]{1,0:T(4,128)}, u32[]{:S(2)}) copy-start(f32[3,256]{1,0:T(4,128)} %get-tuple-element.500) | copy-start | bytes 9220
  558.4 11.0 %copy-start.26 = (f32[3,1,256]{2,0,1:T(4,128)S(1)}, f32[3,1,256]{2,0,1:T(4,128)}, u32[]{:S(2)}) copy-start(f32[3,1,256]{2,0,1:T(4,128)} %copy-done.25) | copy-start | bytes 9220
where the time goes:
time: 580 us; the launch traced here: 575 us
  blocking collectives  211 us (36%)
  local copies, waits for them, and re-layouts  189 us (33%)
  matrix products  99.5 us (17%)
  other arithmetic  57.1 us (10%)
  waiting for transfers between devices  9.53 us (2%)
  starting transfers between devices  6.47 us (1%)
    psum x1, blocking collectives, per_device(): squares = lax.psum(jnp.sum(summed * summed), 'fsdp')  109 us
    dynamic_update_slice x16, local copies, waits for them, and re-layouts, per_device(): lax.scan(forward_block, (zero_state, zero_state, zero_pairs, zero_pairs,...  71.3 us
    psum x1, blocking collectives, per_device(): summed = lax.psum(filter_local, 'ctx')  61.1 us
    gather x2, local copies, waits for them, and re-layouts, per_device(): filter_taps[:, jnp.maximum(lag_index, 0)]  59.7 us
    all_gather x1, blocking collectives, per_device(): everyone = lax.all_gather(local_states[None], 'ctx', axis=0, tiled=True)  41.3 us
    dot_general x8, matrix products, forward_block(): jnp.einsum('kgnt,tgm->kngm', block_moments, e_block, precision=precise)  23.1 us
    dot_general x8, matrix products, forward_block(): jnp.einsum('tgm,sgm->gts', e_block, z_wide, precision=precise)  16.3 us
    unnamed x72, local copies, waits for them, and re-layouts  15.9 us
  transfers between devices with their start and end apart: 2, of which 1 were waited for; matrix products, arithmetic and copies ran while one was open for 14% of the time, Pallas kernels for 0%

commit v1 on v0

--- a/solution.py
+++ b/solution.py
@@ -66,7 +66,11 @@
         3, order_count, channels
     )
     rate_cols = jnp.repeat(decay_rates.T, members, axis=1)
-    everyone = lax.all_gather(local_states[None], "ctx", axis=0, tiled=True)
+    own = local_states[None]
+    n_dev = lax.axis_size("ctx")
+    blocks = jnp.stack([own for _ in range(n_dev)])
+    blocks = lax.all_to_all(blocks, "ctx", split_axis=0, concat_axis=0)
+    everyone = jnp.concatenate(blocks, axis=0)
     device_ids = jnp.arange(ctx_count, dtype=jnp.int32)
     ahead_steps = (ctx_index - 1 - device_ids).astype(jnp.float32)[:, None, None]
     behind_steps = (device_ids - ctx_index - 1).astype(jnp.float32)[:, None, None]

time: 580 us -> 538 us (0.928)
  blocking collectives: 211 us -> 170 us
  starting transfers between devices: 6.47 us -> 12.7 us
    all_gather x1 -> x0, blocking collectives: 41.3 us -> none  [per_device(): everyone = lax.all_gather(local_states[None], 'ctx', axis=0, tiled=True)]
    all_to_all x0 -> x1, starting transfers between devices: none -> 6.39 us  [per_device(): blocks = lax.all_to_all(blocks, 'ctx', split_axis=0, concat_axis=0)]
    unnamed x72 -> x86, local copies, waits for them, and re-layouts: 15.9 us -> 17 us
  transfers between devices with their start and end apart: 2 -> 3, of which waited for: 1 -> 1; matrix products, arithmetic and copies ran while one was open for 14% -> 55% of each run, Pallas kernels for 0% -> 0%
where the time goes in v1:
time: 538 us; the launch traced here: 534 us
  local copies, waits for them, and re-layouts  189 us (35%)
  blocking collectives  170 us (32%)
  matrix products  96.4 us (18%)
  other arithmetic  53.2 us (10%)
  starting transfers between devices  12.7 us (2%)
  waiting for transfers between devices  8.82 us (2%)
    psum x1, blocking collectives, per_device(): squares = lax.psum(jnp.sum(summed * summed), 'fsdp')  105 us
    dynamic_update_slice x16, local copies, waits for them, and re-layouts, per_device(): lax.scan(forward_block, (zero_state, zero_state, zero_pairs, zero_pairs,...  71.2 us
    psum x1, blocking collectives, per_device(): summed = lax.psum(filter_local, 'ctx')  65.8 us
    gather x2, local copies, waits for them, and re-layouts, per_device(): filter_taps[:, jnp.maximum(lag_index, 0)]  60 us
    dot_general x8, matrix products, forward_block(): jnp.einsum('kgnt,tgm->kngm', block_moments, e_block, precision=precise)  23.1 us
    unnamed x86, local copies, waits for them, and re-layouts  17 us
    dot_general x8, matrix products, forward_block(): jnp.einsum('tgm,sgm->gts', e_block, z_wide, precision=precise)  16.3 us
    dot_general x8, matrix products, forward_block(): jnp.einsum('kgns,sgm->kngm', block_ends, z_wide, precision=threepass)  13.8 us
  transfers between devices with their start and end apart: 3, of which 1 were waited for; matrix products, arithmetic and copies ran while one was open for 55% of the time, Pallas kernels for 0%

profile of v1, /device:TPU:1, one launch (start us, length us, event | category | flops | bytes accessed | tf_op | source)
XLA Modules:
  0.0 533.8 jit_solution(9603858495399764068)
XLA Ops:
  2.2 5.0 collective-permute-start
  14.9 54.8 %gather_fusion = f32[16384,16]{1,0:T(8,128)} fusion(f32[16,128]{0,1:T(8,128)S(1)} %copy.79, s32[16384]{0:T(1024)S(1)} %bitcast_clamp_fusion), kind=kCustom, calls=%fused_computation | custom fusion | bytes 2162688 | tf_op jit(solution)/shard_map/gather | solution.py:103
  69.7 5.2 copy.80
  77.6 2.6 copy.75
  80.2 5.5 %rev.26 = f32[16,16,1024]{2,1,0:T(8,128)} reverse(f32[16,16,1024]{2,1,0:T(8,128)} %get-tuple-element.523), dimensions={2} | reverse | bytes 2097152 | tf_op jit(solution)/shard_map/jit(_flip)/rev | solution.py:60
  86.4 2.0 copy.78
  92.2 3.3 rev.29
  95.6 4.9 multiply_add_fusion
  103.1 2.5 fusion.63
  112.1 6.4 %all-to-all-start = ((f32[16,1,3,16,256]{4,3,2,1,0:T(8,128)}), f32[16,1,3,16,256]{4,3,2,1,0:T(8,128)}, u32[]{:S(2)}, u32[]{:S(2)}) async-start(f32[16,1,3,16,256]{4,3,2,1,0:T(8,128)} %stack.62), calls=%async_computation | async-start | bytes 1572864 | tf_op jit(solution)/shard_map/all_to_all | solution.py:72
  121.6 132.4 %while.38 = (s32[]{:T(128)}, f32[16,16,16]{0,2,1:T(8,128)S(1)}, f32[16,16,16]{0,2,1:T(8,128)}, f32[16,16]{0,1:T(8,128)}, f32[16,16]{0,1:T(8,128)}, /*index=5*/f3...) while((s32[]{:T(128)}, f32[16,16,16]{0,2,1:T(8,128)S(1)}, ...), condition=%wide.region_4.5_spmd.clone, body=%wide.region_1.0_spmd.clone.sunk | while | flops 101380864 | bytes 5014714 | solution.py:125
  124.4 2.9 convolution_bitcast_fusion.8
  130.2 4.5 dynamic_update_slice.17
  139.6 2.9 convolution_bitcast_fusion.8
  147.0 4.5 dynamic_update_slice.17
  156.3 2.9 convolution_bitcast_fusion.8
  163.7 4.5 dynamic_update_slice.17
  168.2 2.0 convolution_add_fusion.6
  173.1 2.9 convolution_bitcast_fusion.8
  180.5 4.5 dynamic_update_slice.17
  184.9 2.0 convolution_add_fusion.6
  189.8 2.9 convolution_bitcast_fusion.8
  197.2 4.5 dynamic_update_slice.17
  206.6 2.9 convolution_bitcast_fusion.8
  214.0 4.5 dynamic_update_slice.17
  223.3 2.9 convolution_bitcast_fusion.8
  230.7 4.5 dynamic_update_slice.17
  240.1 2.9 convolution_bitcast_fusion.8
  247.5 4.5 dynamic_update_slice.17
  254.0 5.9 %rev.30 = f32[16,128,128]{2,1,0:T(8,128)} reverse(f32[16,128,128]{2,1,0:T(8,128)S(1)} %get-tuple-element.242), dimensions={2} | reverse | bytes 2097152 | tf_op jit(solution)/shard_map/jit(_flip)/rev | solution.py:18
  264.0 6.2 %reshape.179 = f32[16,128,255]{2,1,0:T(8,128)} reshape(f32[16,32640]{1,0:T(8,128)} %slice.116) | data formatting | bytes 4177920 | tf_op jit(solution)/shard_map/reshape | solution.py:23
  274.3 49.1 %while.39 = (s32[]{:T(128)}, f32[16,16,16]{0,2,1:T(8,128)S(1)}, f32[8,128,16,16]{1,0,3,2:T(8,128)}, f32[16,16,1]{0,1,2:T(8,128)S(1)}, f32[8,128,16,16]{1,3,2,0:T...) while((s32[]{:T(128)}, f32[16,16,16]{0,2,1:T(8,128)S(1)}, ...), condition=%wide.region_7.8_spmd.clone, body=%wide.region_6.7_spmd.clone.sunk | while | flops 62996484 | bytes 2277520 | solution.py:138
  275.5 4.4 dynamic_update_slice.18
  281.6 4.4 dynamic_update_slice.18
  287.8 4.4 dynamic_update_slice.18
  293.9 4.4 dynamic_update_slice.18
  300.0 4.4 dynamic_update_slice.18
  306.1 4.4 dynamic_update_slice.18
  312.2 4.4 dynamic_update_slice.18
  318.3 4.4 dynamic_update_slice.18
  328.0 2.5 fusion.68
  330.6 65.8 %psum.14 = f32[2,16,16]{2,1,0:T(8,128)S(1)} all-reduce(f32[2,16,16]{2,1,0:T(8,128)S(1)} %pad_maximum_fusion.5), channel_id=1, replica_groups=mesh['fsdp'=32,'ctx'=16] {'ctx'}, use_global_device_ids=true, to_apply=%region_15.16 | all-reduce | flops 512 | bytes 4096 | tf_op jit(solution)/shard_map/psum | solution.py:172
  397.0 2.4 reshape.170
  399.4 104.7 %psum.15 = f32[]{:T(128)} all-reduce(f32[]{:T(128)} %multiply_reduce_fusion.6), channel_id=1, replica_groups=mesh['fsdp'=32,'ctx'=16] {'fsdp'}, use_global_device_ids=true, to_apply=%region_17.18 | all-reduce | flops 1 | bytes 8 | tf_op jit(solution)/shard_map/psum | solution.py:173
  510.6 2.3 fusion.69
  517.8 8.8 %collective-permute-done.1 = f32[3,2,256]{1,2,0:T(8,128)} collective-permute-done((f32[3,2,256]{1,2,0:T(8,128)}, f32[3,2,256]{1,2,0:T(8,128)}, u32[]{:S(2)}, u32[]{:S(2)}) %collective-permute-start.1) | collective-permute-done | bytes 6176 | tf_op jit(solution)/shard_map/ppermute | solution.py:13
  527.9 3.3 fusion.54
  531.2 2.6 copy.97
  (231 shorter events, 135.9 us)
Async XLA Ops:
  2.2 93.4 %collective-permute-start = (bf16[3,2,256]{1,2,0:T(8,128)(2,1)}, bf16[3,2,256]{1,2,0:T(8,128)(2,1)}, u32[]{:S(2)}, u32[]{:S(2)}) collective-permute-start(bf16[3,2,256]{1,2,0:T(8,128)(2,1)} %copy.76), channel_id=1, source_target_pairs={{0,1},{1,2},{2,3},{3,4},{4,5},{5,6},{6,7},{7,8},{8,9},{9,10},{10,1... | collective-permute-start | bytes 9224 | tf_op jit(solution)/shard_map/ppermute | solution.py:13
  10.3 4.0 copy-start.16
  10.3 4.4 copy-start.13
  10.3 3.4 copy-start.30
  77.1 8.7 %copy-start.29 = (f32[3,1,256]{2,1,0:T(1,128)S(1)}, f32[3,1,256]{2,1,0:T(1,128)}, u32[]{:S(2)}) copy-start(f32[3,1,256]{2,1,0:T(1,128)} %get-tuple-element.511) | copy-start | bytes 9220
  77.6 10.8 %copy-start.28 = (f32[16,16]{0,1:T(8,128)S(1)}, f32[16,16]{0,1:T(8,128)}, u32[]{:S(2)}) copy-start(f32[16,16]{0,1:T(8,128)} %get-tuple-element.517) | copy-start | bytes 3076
  100.5 1.6 copy-start
  100.5 2.6 copy-start.6
  100.5 2.7 copy-start.7
  108.1 10.6 %copy-start.1 = (f32[1024,256]{0,1:T(8,128)}, f32[1024,256]{0,1:T(8,128)S(1)}, u32[]{:S(2)}) copy-start(f32[1024,256]{0,1:T(8,128)S(1)} %convert_multiply_fusion.1) | copy-start | bytes 3145732
  109.7 9.3 %copy-start.9 = (f32[16,16,16]{2,1,0:T(8,128)}, f32[16,16,16]{2,1,0:T(8,128)S(1)}, u32[]{:S(2)}) copy-start(f32[16,16,16]{2,1,0:T(8,128)S(1)} %fusion.75) | copy-start | bytes 49156
  112.1 212.9 %all-to-all-start = ((f32[16,1,3,16,256]{4,3,2,1,0:T(8,128)}), f32[16,1,3,16,256]{4,3,2,1,0:T(8,128)}, u32[]{:S(2)}, u32[]{:S(2)}) async-start(f32[16,1,3,16,256]{4,3,2,1,0:T(8,128)} %stack.62), calls=%async_computation | async-start | bytes 1572864 | tf_op jit(solution)/shard_map/all_to_all | solution.py:72
  118.5 1.0 copy-start.8
  264.0 8.1 %copy-start.14 = (f32[16,16]{1,0:T(8,128)S(1)}, f32[16,16]{1,0:T(8,128)}, u32[]{:S(2)}) copy-start(f32[16,16]{1,0:T(8,128)} %get-tuple-element.785) | copy-start | bytes 3076
  264.0 9.0 %copy-start.17 = (f32[16,16]{1,0:T(8,128)S(1)}, f32[16,16]{1,0:T(8,128)}, u32[]{:S(2)}) copy-start(f32[16,16]{1,0:T(8,128)} %get-tuple-element.786) | copy-start | bytes 3076
  274.2 50.8 %copy-start.19 = (f32[16,256]{1,0:T(8,128)S(1)}, f32[16,256]{1,0:T(8,128)}, u32[]{:S(2)}) copy-start(f32[16,256]{1,0:T(8,128)} %neg.32) | copy-start | bytes 49156
  274.2 50.8 %copy-start.32 = (pred[16]{0:T(512)(128)(4,1)S(1)}, pred[16]{0:T(512)(128)(4,1)}, u32[]{:S(2)}) copy-start(pred[16]{0:T(512)(128)(4,1)} %get-tuple-element.531) | copy-start | bytes 52
  274.2 50.8 %copy-start.33 = (pred[16]{0:T(512)(128)(4,1)S(1)}, pred[16]{0:T(512)(128)(4,1)}, u32[]{:S(2)}) copy-start(pred[16]{0:T(512)(128)(4,1)} %get-tuple-element.532) | copy-start | bytes 52
  274.2 50.8 %copy-start.34 = (f32[16]{0:T(128)S(1)}, f32[16]{0:T(128)}, u32[]{:S(2)}) copy-start(f32[16]{0:T(128)} %get-tuple-element.529) | copy-start | bytes 196
  274.3 50.8 %copy-start.35 = (f32[16]{0:T(128)S(1)}, f32[16]{0:T(128)}, u32[]{:S(2)}) copy-start(f32[16]{0:T(128)} %get-tuple-element.530) | copy-start | bytes 196
  274.3 50.8 %copy-start.36 = (f32[16]{0:T(128)S(1)}, f32[16]{0:T(128)}, u32[]{:S(2)}) copy-start(f32[16]{0:T(128)} %maximum_multiply_fusion) | copy-start | bytes 196
  323.4 4.5 copy-start.10
  323.4 4.5 copy-start.27
  323.4 4.6 copy-start.2
  323.4 4.6 copy-start.15
  323.4 4.6 copy-start.31
  323.5 7.0 %copy-start.11 = (f32[16,16]{0,1:T(8,128)S(1)}, f32[16,16]{0,1:T(8,128)}, u32[]{:S(2)}) copy-start(f32[16,16]{0,1:T(8,128)} %get-tuple-element.241) | copy-start | bytes 3076
  323.5 7.0 %copy-start.12 = (f32[16,16]{0,1:T(8,128)S(1)}, f32[16,16]{0,1:T(8,128)}, u32[]{:S(2)}) copy-start(f32[16,16]{0,1:T(8,128)} %get-tuple-element.243) | copy-start | bytes 3076
  323.5 7.0 %copy-start.23 = (f32[16,16]{1,0:T(8,128)S(1)}, f32[16,16]{1,0:T(8,128)}, u32[]{:S(2)}) copy-start(f32[16,16]{1,0:T(8,128)} %get-tuple-element.443) | copy-start | bytes 3076
  323.5 7.0 %copy-start.24 = (f32[16,16]{1,0:T(8,128)S(1)}, f32[16,16]{1,0:T(8,128)}, u32[]{:S(2)}) copy-start(f32[16,16]{1,0:T(8,128)} %get-tuple-element.444) | copy-start | bytes 3076
  323.5 7.0 %copy-start.25 = (f32[16,16]{1,0:T(8,128)S(1)}, f32[16,16]{1,0:T(8,128)}, u32[]{:S(2)}) copy-start(f32[16,16]{1,0:T(8,128)} %param.11) | copy-start | bytes 3076
  323.5 7.0 %copy-start.26 = (f32[16,16]{1,0:T(8,128)S(1)}, f32[16,16]{1,0:T(8,128)}, u32[]{:S(2)}) copy-start(f32[16,16]{1,0:T(8,128)} %param.12) | copy-start | bytes 3076
  325.0 180.5 %copy-start.4 = (f32[16,16,1024]{2,1,0:T(8,128)S(1)}, f32[16,16,1024]{2,1,0:T(8,128)}, u32[]{:S(2)}) copy-start(f32[16,16,1024]{2,1,0:T(8,128)} %rev.29) | copy-start | bytes 3145732
  507.3 2.0 copy-start.5
  507.3 2.0 copy-start.18
  507.3 3.2 copy-start.3
  513.9 12.8 %collective-permute-start.1 = (f32[3,2,256]{1,2,0:T(8,128)}, f32[3,2,256]{1,2,0:T(8,128)}, u32[]{:S(2)}, u32[]{:S(2)}) collective-permute-start(f32[3,2,256]{1,2,0:T(8,128)} %slice.113), channel_id=1, source_target_pairs={{1,0},{2,1},{3,2},{4,3},{5,4},{6,5},{7,6},{8,7},{9,8},{10,9},{11,1... | collective-permute-start | bytes 18440 | tf_op jit(solution)/shard_map/ppermute | solution.py:13
  517.8 10.1 %copy-start.20 = (f32[3,256]{1,0:T(4,128)S(1)}, f32[3,256]{1,0:T(4,128)}, u32[]{:S(2)}) copy-start(f32[3,256]{1,0:T(4,128)} %get-tuple-element.527) | copy-start | bytes 9220
  517.8 10.1 %copy-start.21 = (f32[3,256]{1,0:T(4,128)S(1)}, f32[3,256]{1,0:T(4,128)}, u32[]{:S(2)}) copy-start(f32[3,256]{1,0:T(4,128)} %get-tuple-element.528) | copy-start | bytes 9220
  517.8 10.1 %copy-start.22 = (f32[3,1,256]{2,0,1:T(4,128)S(1)}, f32[3,1,256]{2,0,1:T(4,128)}, u32[]{:S(2)}) copy-start(f32[3,1,256]{2,0,1:T(4,128)} %copy.132) | copy-start | bytes 9220
